TPU v7x, 32 devices: a whole 2x2x4 slice. The times are simulated.
32 devices in a mesh: mem: 4 (over y, core), lat: 2 (over x), lon: 4 (over z).
Axes of the slice: x: 2, y: 2, z: 4, core: 2. Of those that a mesh axis runs over, the one named last changes fastest.
Arguments:
- perturbations: bfloat16 [8, 4, 768, 1536], P('mem', None, 'lat', 'lon'), may hold values from -2 to 2
- innovation: float32 [2, 8192], P('lat', 'lon'), may hold values from -4.2 to 4.2
- obs_weight: float32 [2, 8192], P('lat', 'lon'), may hold values from 0.5 to 6, as said below
- obs_cell: int32 [2, 8192], P('lat', 'lon'), may hold values from 0 to 147455
- obs_level: int32 [2, 8192], P('lat', 'lon'), may hold values from 0 to 3
- cutoff: int32 [4], replicated, may hold values from 16 to 127
Outputs:
- solution: float32 [8, 4, 768, 512], P('mem', None, ('lat', 'lon'))
- residual: float32 [8, 4, 768, 512], P('mem', None, ('lat', 'lon'))
Inputs may be any that keep to these rules, and one draw needn't show every extreme that they name: `obs_weight`: positive weights.
All inputs are finite; a program needn't handle non-finite values.
Results may differ from a plain program's by a relative error of at most 0.0008.
Values may be sent and summed in bfloat16 or wider, within the bound.
No kernel may reach another device: no remote copies, remote signals or barrier semaphores. Data moves between devices by JAX's collectives and lax.ppermute only.
A program may use at most 64 MiB of HBM per device.

v0:
```python
import jax
import jax.numpy as jnp
from jax import lax
from jax.sharding import PartitionSpec as P

NLON = 1536
KMAX = 256
ITERS = 2


def basis_table(transposed):
    factor = 2.0 * jnp.pi / NLON
    if transposed:
        columns = jnp.arange(NLON, dtype=jnp.int32)[None, :]
        cos_waves = jnp.arange(KMAX, dtype=jnp.int32)[:, None]
        axis_join = 0
    else:
        columns = jnp.arange(NLON, dtype=jnp.int32)[:, None]
        cos_waves = jnp.arange(KMAX, dtype=jnp.int32)[None, :]
        axis_join = 1
    cos_phase = (columns * cos_waves % NLON).astype(jnp.float32) * factor
    sin_phase = (columns * (cos_waves + 1) % NLON).astype(jnp.float32) * factor
    joined = jnp.concatenate([jnp.cos(cos_phase), jnp.sin(sin_phase)], axis=axis_join)
    return joined / jnp.sqrt(jnp.float32(KMAX))


def spectrum_of(cutoff):
    wavenumbers = jnp.concatenate(
        [jnp.arange(KMAX, dtype=jnp.float32), jnp.arange(1, KMAX + 1, dtype=jnp.float32)]
    )
    scaled = wavenumbers[None, :] / cutoff.astype(jnp.float32)[:, None]
    return 1.0 / (1.0 + scaled * scaled)


def member_total(partial_value):
    return lax.psum(partial_value, "mem")


def norm_total(residual):
    return lax.psum(jnp.sum(residual * residual), ("mem", "lat", "lon"))


def body(perturbations, innovation, obs_weight, obs_cell, obs_level, cutoff):
    members_here, levels, tile_rows, tile_cols = perturbations.shape
    line_rows = tile_rows // lax.axis_size("lon")
    basis_rows = basis_table(False)
    basis_cols = basis_table(True)
    spectrum = spectrum_of(cutoff)
    located = (obs_level * (tile_rows * tile_cols) + obs_cell).reshape(-1)
    weights = obs_weight.reshape(-1)

    def gridded_of(weighted):
        field = jnp.zeros((levels * tile_rows * tile_cols,), jnp.float32).at[located].add(weighted)
        return field.reshape(levels, tile_rows, tile_cols)

    def analyse(products):
        summed = jnp.dot(
            products.reshape(-1, NLON),
            basis_rows,
            precision=lax.Precision.HIGHEST,
            preferred_element_type=jnp.float32,
        )
        return (
            summed.reshape(members_here, levels, line_rows, 2 * KMAX) * spectrum[None, :, None, :]
        )

    line_pert = lax.all_to_all(perturbations, "lon", split_axis=2, concat_axis=3, tiled=True)

    def adjoint_part(gridded):
        grid_lines = lax.all_to_all(gridded, "lon", split_axis=1, concat_axis=2, tiled=True)
        products = line_pert.astype(jnp.float32) * grid_lines[None]
        return analyse(products)

    right_side = adjoint_part(gridded_of(weights * innovation.reshape(-1)))
    solution = jnp.zeros_like(right_side)
    residual = right_side
    direction = right_side
    norm_now = norm_total(residual)
    for iteration in range(ITERS):
        coeffs = direction * spectrum[None, :, None, :]
        synthesized = jnp.dot(
            coeffs.reshape(-1, 2 * KMAX),
            basis_cols,
            precision=lax.Precision.HIGHEST,
            preferred_element_type=jnp.float32,
        )
        forward_synthesized = synthesized.reshape(members_here, levels, line_rows, NLON)
        partial_value = jnp.sum(line_pert.astype(jnp.float32) * forward_synthesized, axis=0)
        on_tiles = lax.all_to_all(partial_value, "lon", split_axis=2, concat_axis=1, tiled=True)
        increment = member_total(on_tiles)
        sampled = increment.reshape(-1)[located]
        image = direction + adjoint_part(gridded_of(weights * sampled))
        curvature = lax.psum(jnp.sum(direction * image), ("mem", "lat", "lon"))
        step_size = norm_now / curvature
        solution = solution + step_size * direction
        residual = residual - step_size * image
        if iteration + 1 < ITERS:
            norm_next = norm_total(residual)
            direction = residual + norm_next / norm_now * direction
            norm_now = norm_next
    return (solution, residual)


def solution(mesh):
    placed = (
        P("mem", None, "lat", "lon"),
        P("lat", "lon"),
        P("lat", "lon"),
        P("lat", "lon"),
        P("lat", "lon"),
        P(),
    )
    return jax.shard_map(
        body,
        mesh=mesh,
        in_specs=placed,
        out_specs=(P("mem", None, ("lat", "lon"), None), P("mem", None, ("lat", "lon"), None)),
        check_vma=False,
    )
```

profile of v0, /device:TPU:0, one launch (start us, length us, event | category | flops | bytes accessed | tf_op | source)
XLA Modules:
  0.0 842.8 jit_solution(17484831876931123835)
XLA Ops:
  7.2 0.7 mul.200
  7.9 0.7 compare_select_fusion
  8.6 12.8 %scatter_custom_fusion = f32[589824]{0:T(1024)} fusion(s32[2048]{0:T(1024)S(1)} %bitcast.74, f32[2048]{0:T(1024)S(1)} %mul.200, f32[]{:T(128)} %constant.20.clone.1), kind=kCustom, calls=%fused_computation.75 | custom fusion | flops 2048 | bytes 2359300 | tf_op jit(solution)/shard_map/scatter-add | solution.py:53
  21.4 3.4 reshape.134
  24.8 4.6 copy.45
  29.4 6.3 all-to-all-start.1
  35.7 4.9 copy.43
  40.6 49.0 %all-to-all-done.1 = f32[4,384,384]{2,0,1:T(4,128)} async-done(((f32[4,384,384]{2,0,1:T(4,128)}), f32[4,384,384]{2,0,1:T(4,128)}, u32[]{:S(2)}, u32[]{:S(2)}) %all-to-all-start.1) | async-done | bytes 2359328 | tf_op jit(solution)/shard_map/all_to_all | solution.py:70
  89.6 4.5 all-to-all-start
  94.1 0.2 all-reduce.4.cloned.1.call-start
  94.4 0.1 fusion.65
  94.5 5.9 fusion.18
  100.4 8.1 fusion.24
  108.5 6.8 fusion.21
  115.3 7.0 fusion.27
  122.3 1.8 copy.46
  124.2 1.8 copy.66
  125.9 21.6 %all-to-all-done = bf16[2,4,384,384]{3,1,0,2:T(4,128)(2,1)} async-done(((bf16[2,4,384,384]{3,1,0,2:T(4,128)(2,1)}), bf16[2,4,384,384]{3,1,0,2:T(4,128)(2,1)}, u32[]{:S(2)}, u32[]{:S(2)}) %all-to-all-start) | async-done | bytes 2359328 | tf_op jit(solution)/shard_map/all_to_all | solution.py:67
  147.6 5.7 copy.70
  153.3 6.4 reshape.141
  159.6 10.9 %fusion.47 = f32[2,4,96,512]{3,2,1,0:T(8,128)S(1)} fusion(f32[1536,256]{1,0:T(8,128)} %fusion.21, f32[1536,256]{1,0:T(8,128)S(1)} %fusion.18, f32[2,4,96,1536]{3,2,1,0:T(8,128)} %reshape.141, f32[4,96,1536]{2,1,0:T(8,128)} %bitcast.63, f32[4,512]{1,0:T(4,128)S(1)} %fusion.65), kind=kOutput, calls=%fused_computation.70 | convolution fusion | flops 7250903040 | bytes 11804672 | tf_op jit(solution)/shard_map/dot_general | solution.py:57
  170.6 10.3 %multiply_reduce_fusion.1 = f32[4,96,1536]{2,1,0:T(8,128)} fusion(f32[2,4,96,1536]{3,2,1,0:T(8,128)S(1)} %copy-done, f32[256,1536]{1,0:T(8,128)S(1)} %copy-done.10, f32[256,1536]{1,0:T(8,128)S(1)} %copy-done.8, f32[2,4,96,512]{3,2,1,0:T(8,128)S(1)} %fusion.47, f32[4,512]{1,0:T(4,128)S(1)} %fusion.65), kind=kOutput, calls=%fused_computation.11 | convolution fusion | flops 7251492864 | bytes 11804672 | tf_op jit(solution)/shard_map/dot_general | solution.py:81
  180.9 4.5 copy.48
  185.4 75.5 %all_to_all.90 = f32[4,96,1536]{1,0,2:T(4,128)} all-to-all(f32[4,96,1536]{1,0,2:T(4,128)} %copy.48), channel_id=1, replica_groups=mesh['mem'=4,'lat'=2,'lon'=4] {'lon'}, dimensions={2} | all-to-all | bytes 4718592 | tf_op jit(solution)/shard_map/all_to_all | solution.py:89
  261.0 4.7 copy.50
  265.6 3.2 reshape.135
  269.0 54.8 %all-reduce.4.cloned.1.call-done = f32[589824]{0:T(1024)} async-done(((f32[589824]{0:T(1024)}), f32[589824]{0:T(1024)}) %all-reduce.4.cloned.1.call-update) | async-done | bytes 2359312 | tf_op jit(solution)/shard_map/psum | solution.py:36
  323.8 24.5 %gather_fusion = f32[2048]{0:T(1024)S(1)} fusion(f32[589824]{0:T(1024)} %all-reduce.4.cloned.1.call-done, s32[2048]{0:T(1024)S(1)} %broadcast_clamp_fusion), kind=kCustom, calls=%fused_computation | custom fusion | bytes 24576 | tf_op jit(solution)/shard_map/gather | solution.py:91
  348.3 12.8 %scatter_custom_fusion.1 = f32[589824]{0:T(1024)} fusion(s32[2048]{0:T(1024)S(1)} %bitcast.76, f32[2048]{0:T(1024)S(1)} %mul.226, f32[]{:T(128)} %constant.20.clone.1), kind=kCustom, calls=%fused_computation.73 | custom fusion | flops 2048 | bytes 2359300 | tf_op jit(solution)/shard_map/scatter-add | solution.py:53
  361.1 3.4 reshape.136
  364.5 3.2 copy.51
  367.7 58.7 %all_to_all.91 = f32[4,384,384]{2,0,1:T(4,128)S(1)} all-to-all(f32[4,384,384]{2,0,1:T(4,128)S(1)} %copy.51), channel_id=1, replica_groups=mesh['mem'=4,'lat'=2,'lon'=4] {'lon'}, dimensions={1} | all-to-all | bytes 4718592 | tf_op jit(solution)/shard_map/all_to_all | solution.py:70
  426.4 0.2 copy.52
  426.6 0.3 copy.67
  426.9 0.5 slice-done.1
  427.5 0.6 copy-done.2
  428.0 0.5 copy-done.4
  428.5 8.6 %multiply_reduce_fusion.4 = (f32[]{:T(128)}, f32[]{:T(128)}, f32[2,4,96,512]{3,2,1,0:T(8,128)S(1)}) fusion(f32[2,4,96,512]{3,2,1,0:T(8,128)S(1)} %fusion.47, f32[4,512]{1,0:T(4,128)S(1)} %fusion.65, f32[1536,256]{1,0:T(8,128)S(1)} %copy-done.4, f32[1536,256]{1,0:T(8,128)S(1)} %copy-done.2, f32[2,4,96,1536]{3,2,1,0:T(8,128)S(1)} %bitcast.59, ...), kind=kOutput, calls=%fused_computation.45 | convolution fusion | flops 7252869120 | bytes 13377544 | tf_op jit(solution)/shard_map/dot_general | solution.py:57
  437.1 38.3 %all-reduce = (f32[]{:T(128)}, f32[]{:T(128)}) all-reduce(f32[]{:T(128)} %get-tuple-element.3, f32[]{:T(128)} %get-tuple-element.2), channel_id=1, replica_groups=mesh['mem'=4,'lat'=2,'lon'=4] {'mem','lat','lon'}, use_global_device_ids=true, to_apply=%region_2.3 | all-reduce | flops 2 | bytes 16 | tf_op jit(solution)/shard_map/psum | solution.py:40
  476.8 1.1 multiply_reduce_fusion.3
  477.9 41.6 %psum.45 = f32[]{:T(128)} all-reduce(f32[]{:T(128)} %multiply_reduce_fusion.3), channel_id=1, replica_groups=mesh['mem'=4,'lat'=2,'lon'=4] {'mem','lat','lon'}, use_global_device_ids=true, to_apply=%region_9.10 | all-reduce | flops 1 | bytes 8 | tf_op jit(solution)/shard_map/psum | solution.py:40
  520.8 0.4 multiply_add_fusion.2
  521.2 1.2 copy-done.6
  522.4 0.8 copy-done.11
  523.2 11.4 %multiply_reduce_fusion = f32[4,96,1536]{2,1,0:T(8,128)} fusion(f32[2,4,96,1536]{3,2,1,0:T(8,128)} %reshape.141, f32[256,1536]{1,0:T(8,128)S(1)} %copy-done.11, f32[256,1536]{1,0:T(8,128)S(1)} %copy-done.9, f32[2,4,96,512]{3,2,1,0:T(8,128)S(1)} %multiply_add_fusion.2, f32[4,512]{1,0:T(4,128)S(1)} %fusion.65), kind=kOutput, calls=%fused_computation.8 | convolution fusion | flops 7251492864 | bytes 11804672 | tf_op jit(solution)/shard_map/dot_general | solution.py:81
  534.6 4.5 copy.54
  539.1 75.7 %all_to_all.92 = f32[4,96,1536]{1,0,2:T(4,128)} all-to-all(f32[4,96,1536]{1,0,2:T(4,128)} %copy.54), channel_id=1, replica_groups=mesh['mem'=4,'lat'=2,'lon'=4] {'lon'}, dimensions={2} | all-to-all | bytes 4718592 | tf_op jit(solution)/shard_map/all_to_all | solution.py:89
  614.8 4.6 copy.56
  619.4 3.2 reshape.137
  622.7 54.8 %all-reduce.6.cloned.1.call-done = f32[589824]{0:T(1024)} async-done(((f32[589824]{0:T(1024)}), f32[589824]{0:T(1024)}) %all-reduce.6.cloned.1.call-update) | async-done | bytes 2359312 | tf_op jit(solution)/shard_map/psum | solution.py:36
  677.4 24.5 %gather_fusion.1 = f32[2048]{0:T(1024)S(1)} fusion(f32[589824]{0:T(1024)} %all-reduce.6.cloned.1.call-done, s32[2048]{0:T(1024)S(1)} %broadcast_clamp_fusion), kind=kCustom, calls=%fused_computation.1 | custom fusion | bytes 24576 | tf_op jit(solution)/shard_map/gather | solution.py:91
  701.9 12.8 %scatter_custom_fusion.2 = f32[589824]{0:T(1024)} fusion(s32[2048]{0:T(1024)S(1)} %bitcast.77, f32[2048]{0:T(1024)S(1)} %mul.240, f32[]{:T(128)} %constant.20.clone.1), kind=kCustom, calls=%fused_computation.71 | custom fusion | flops 2048 | bytes 2359300 | tf_op jit(solution)/shard_map/scatter-add | solution.py:53
  714.7 3.4 reshape.138
  718.1 3.2 copy.57
  721.3 58.4 %all_to_all.93 = f32[4,384,384]{2,0,1:T(4,128)S(1)} all-to-all(f32[4,384,384]{2,0,1:T(4,128)S(1)} %copy.57), channel_id=1, replica_groups=mesh['mem'=4,'lat'=2,'lon'=4] {'lon'}, dimensions={1} | all-to-all | bytes 4718592 | tf_op jit(solution)/shard_map/all_to_all | solution.py:70
  779.7 0.2 copy.58
  779.9 0.3 copy.68
  780.3 0.5 slice-done.3
  780.8 0.6 copy-done.3
  781.4 0.5 copy-done.5
  781.8 0.5 copy-done.7
  782.3 9.5 %multiply_reduce_fusion.2 = (f32[]{:T(128)}, f32[2,4,96,512]{3,2,1,0:T(8,128)}) fusion(f32[2,4,96,512]{3,2,1,0:T(8,128)S(1)} %copy-done.7, f32[4,512]{1,0:T(4,128)S(1)} %fusion.65, f32[1536,256]{1,0:T(8,128)S(1)} %copy-done.5, f32[1536,256]{1,0:T(8,128)S(1)} %copy-done.3, f32[2,4,96,1536]{3,2,1,0:T(8,128)S(1)} %bitcast.61, f32[4,96,1536]{2,1,0:T(8,128)S(1)} %bitcast.64), kind=kOutput, calls=%fused_computation.39 | convolution fusion | flops 7252082688 | bytes 13377540 | tf_op jit(solution)/shard_map/dot_general | solution.py:57
  791.8 38.3 %psum.47 = f32[]{:T(128)} all-reduce(f32[]{:T(128)} %get-tuple-element.9), channel_id=1, replica_groups=mesh['mem'=4,'lat'=2,'lon'=4] {'mem','lat','lon'}, use_global_device_ids=true, to_apply=%region_14.15 | all-reduce | flops 1 | bytes 8 | tf_op jit(solution)/shard_map/psum | solution.py:93
  831.4 4.3 multiply_subtract_fusion
  (40 shorter events, 0.2 us)
Async XLA Ops:
  29.4 60.3 %all-to-all-start.1 = ((f32[4,384,384]{2,0,1:T(4,128)}), f32[4,384,384]{2,0,1:T(4,128)}, u32[]{:S(2)}, u32[]{:S(2)}) async-start(f32[4,384,384]{2,0,1:T(4,128)} %copy.45), calls=%async_computation.1 | async-start | bytes 4718592 | tf_op jit(solution)/shard_map/all_to_all | solution.py:70
  40.6 53.8 %copy-start.13 = (s32[4]{0:T(128)S(1)}, s32[4]{0:T(128)}, u32[]{:S(2)}) copy-start(s32[4]{0:T(128)} %param.11) | copy-start | bytes 52
  89.6 57.9 %all-to-all-start = ((bf16[2,4,384,384]{3,1,0,2:T(4,128)(2,1)}), bf16[2,4,384,384]{3,1,0,2:T(4,128)(2,1)}, u32[]{:S(2)}, u32[]{:S(2)}) async-start(bf16[2,4,384,384]{3,1,0,2:T(4,128)(2,1)} %copy.43), calls=%async_computation | async-start | bytes 4718592 | tf_op jit(solution)/shard_map/all_to_all | solution.py:67
  94.1 229.7 %all-reduce.4.cloned.1.call-start = ((), (), s32[]{:S(2)}) async-start(), calls=%async_computation.6 | async-start | bytes 4718592 | tf_op jit(solution)/shard_map/psum | solution.py:36
  100.4 59.2 %copy-start.1 = (f32[1536,256]{1,0:T(8,128)}, f32[1536,256]{1,0:T(8,128)S(1)}, u32[]{:S(2)}) copy-start(f32[1536,256]{1,0:T(8,128)S(1)} %fusion.18) | copy-start | bytes 4718596
  159.6 10.9 %copy-start = (f32[2,4,96,1536]{3,2,1,0:T(8,128)S(1)}, f32[2,4,96,1536]{3,2,1,0:T(8,128)}, u32[]{:S(2)}) copy-start(f32[2,4,96,1536]{3,2,1,0:T(8,128)} %reshape.141) | copy-start | bytes 14155780
  159.6 10.9 %copy-start.8 = (f32[256,1536]{1,0:T(8,128)S(1)}, f32[256,1536]{1,0:T(8,128)}, u32[]{:S(2)}) copy-start(f32[256,1536]{1,0:T(8,128)} %fusion.24) | copy-start | bytes 4718596
  159.6 11.0 %copy-start.10 = (f32[256,1536]{1,0:T(8,128)S(1)}, f32[256,1536]{1,0:T(8,128)}, u32[]{:S(2)}) copy-start(f32[256,1536]{1,0:T(8,128)} %fusion.27) | copy-start | bytes 4718596
  268.9 408.5 %all-reduce.6.cloned.1.call-start = ((), (), s32[]{:S(2)}) async-start(), calls=%async_computation.7 | async-start | bytes 4718592 | tf_op jit(solution)/shard_map/psum | solution.py:36
  268.9 79.3 %copy-start.12 = (f32[1,2048]{1,0:T(1,128)S(1)}, f32[1,2048]{1,0:T(1,128)}, u32[]{:S(2)}) copy-start(f32[1,2048]{1,0:T(1,128)} %param.8) | copy-start | bytes 24580
  367.7 59.2 %slice-start = ((s8[4718592]{0:T(1024)(128)(4,1)}), s8[4194304]{0:T(1024)(128)(4,1)S(1)}, s32[]{:S(2)}) async-start(s8[4718592]{0:T(1024)(128)(4,1)} %bitcast.58), calls=%async_computation.8 | async-start | bytes 8388608
  426.4 1.0 slice-start.1
  426.6 1.4 copy-start.2
  426.6 1.9 copy-start.4
  520.8 1.6 copy-start.9
  520.8 2.4 copy-start.11
  521.2 1.2 copy-start.6
  721.3 59.0 %slice-start.2 = ((s8[4718592]{0:T(1024)(128)(4,1)}), s8[4194304]{0:T(1024)(128)(4,1)S(1)}, s32[]{:S(2)}) async-start(s8[4718592]{0:T(1024)(128)(4,1)} %bitcast.60), calls=%async_computation.10 | async-start | bytes 8388608
  779.7 1.0 slice-start.3
  779.9 1.4 copy-start.3
  779.9 1.9 copy-start.5
  779.9 2.4 copy-start.7
Sparse Core Ops, SparseCore 0:
  269.0 54.7 all-reduce.3
  622.8 54.5 all-reduce.5
where the time goes:
time: 851 us; the launch traced here: 843 us
  blocking collectives  387 us (45%)
  waiting for transfers between devices  180 us (21%)
  local copies, waits for them, and re-layouts  122 us (14%)
  other arithmetic  73.6 us (9%)
  matrix products  50.7 us (6%)
  between operations  18.6 us (2%)
  starting transfers between devices  11.1 us (1%)
    all_to_all x2, blocking collectives, body(): lax.all_to_all(partial_value, 'lon', split_axis=2, concat_axis=1, tiled=T...  151 us
    all_to_all x2, blocking collectives, adjoint_part(): lax.all_to_all(gridded, 'lon', split_axis=1, concat_axis=2, tiled=True)  117 us
    psum x2, waiting for transfers between devices, member_total(): return lax.psum(partial_value, 'mem')  110 us
    psum x2, blocking collectives, norm_total(): return lax.psum(jnp.sum(residual * residual), ('mem', 'lat', 'lon'))  79.9 us
    all_to_all x1, waiting for transfers between devices, adjoint_part(): lax.all_to_all(gridded, 'lon', split_axis=1, concat_axis=2, tiled=True)  49 us
    gather x2, local copies, waits for them, and re-layouts, body(): sampled = increment.reshape(-1)[located]  49 us
    scatter-add x3, other arithmetic, gridded_of(): jnp.zeros((levels * tile_rows * tile_cols,), jnp.float32).at[located]  38.4 us
    psum x1, blocking collectives, body(): curvature = lax.psum(jnp.sum(direction * image), ('mem', 'lat', 'lon'))  38.3 us
  transfers between devices with their start and end apart: 4, of which 4 were waited for; matrix products, arithmetic and copies ran while one was open for 4% of the time, Pallas kernels for 0%

commit v1 on v0

--- a/solution.py
+++ b/solution.py
@@ -86,7 +86,12 @@
         )
         forward_synthesized = synthesized.reshape(members_here, levels, line_rows, NLON)
         partial_value = jnp.sum(line_pert.astype(jnp.float32) * forward_synthesized, axis=0)
-        on_tiles = lax.all_to_all(partial_value, "lon", split_axis=2, concat_axis=1, tiled=True)
+        on_tiles = jnp.concatenate(
+            lax.all_to_all(
+                jnp.stack(jnp.split(partial_value, lax.axis_size("lon"), axis=2)), "lon", 0, 0
+            ),
+            axis=1,
+        )
         increment = member_total(on_tiles)
         sampled = increment.reshape(-1)[located]
         image = direction + adjoint_part(gridded_of(weights * sampled))

time: 851 us -> 793 us (0.932)
  blocking collectives: 387 us -> 347 us
  local copies, waits for them, and re-layouts: 122 us -> 107 us
    all_to_all x2, blocking collectives: 151 us -> 112 us  [body(): lax.all_to_all(jnp.stack(jnp.split(partial_value, lax.axis_size('lon'), a...]
    all_to_all x2 -> x0, local copies, waits for them, and re-layouts: 9.27 us -> none  [body(): lax.all_to_all(partial_value, 'lon', split_axis=2, concat_axis=1, tiled=T...]
    reduce_sum x2 -> x0, local copies, waits for them, and re-layouts: 9 us -> none  [body(): jnp.sum(line_pert.astype(jnp.float32) * forward_synthesized, axis=0)]
  transfers between devices with their start and end apart: 4 -> 4, of which waited for: 4 -> 4; matrix products, arithmetic and copies ran while one was open for 4% -> 5% of each run, Pallas kernels for 0% -> 0%
where the time goes in v1:
time: 793 us; the launch traced here: 786 us
  blocking collectives  347 us (44%)
  waiting for transfers between devices  180 us (23%)
  local copies, waits for them, and re-layouts  107 us (13%)
  other arithmetic  73.9 us (9%)
  matrix products  48.3 us (6%)
  between operations  18.2 us (2%)
  starting transfers between devices  11.1 us (1%)
    all_to_all x2, blocking collectives, adjoint_part(): lax.all_to_all(gridded, 'lon', split_axis=1, concat_axis=2, tiled=True)  117 us
    all_to_all x2, blocking collectives, body(): lax.all_to_all(jnp.stack(jnp.split(partial_value, lax.axis_size('lon'), a...  112 us
    psum x2, waiting for transfers between devices, member_total(): return lax.psum(partial_value, 'mem')  110 us
    psum x2, blocking collectives, norm_total(): return lax.psum(jnp.sum(residual * residual), ('mem', 'lat', 'lon'))  79.8 us
    all_to_all x1, waiting for transfers between devices, adjoint_part(): lax.all_to_all(gridded, 'lon', split_axis=1, concat_axis=2, tiled=True)  49 us
    gather x2, local copies, waits for them, and re-layouts, body(): sampled = increment.reshape(-1)[located]  49 us
    scatter-add x3, other arithmetic, gridded_of(): jnp.zeros((levels * tile_rows * tile_cols,), jnp.float32).at[located]  38.4 us
    psum x1, blocking collectives, body(): curvature = lax.psum(jnp.sum(direction * image), ('mem', 'lat', 'lon'))  38.3 us
  transfers between devices with their start and end apart: 4, of which 4 were waited for; matrix products, arithmetic and copies ran while one was open for 5% of the time, Pallas kernels for 0%

profile of v1, /device:TPU:0, one launch (start us, length us, event | category | flops | bytes accessed | tf_op | source)
XLA Modules:
  0.0 785.6 jit_solution(11554780191326104)
XLA Ops:
  7.2 0.7 mul.200
  7.9 0.7 compare_select_fusion
  8.6 12.8 %scatter_custom_fusion = f32[589824]{0:T(1024)} fusion(s32[2048]{0:T(1024)S(1)} %bitcast.84, f32[2048]{0:T(1024)S(1)} %mul.200, f32[]{:T(128)} %constant.20.clone.1), kind=kCustom, calls=%fused_computation.77 | custom fusion | flops 2048 | bytes 2359300 | tf_op jit(solution)/shard_map/scatter-add | solution.py:53
  21.4 3.4 reshape.146
  24.8 4.6 copy.38
  29.4 6.3 all-to-all-start.1
  35.7 4.9 copy.36
  40.6 49.0 %all-to-all-done.1 = f32[4,384,384]{2,0,1:T(4,128)} async-done(((f32[4,384,384]{2,0,1:T(4,128)}), f32[4,384,384]{2,0,1:T(4,128)}, u32[]{:S(2)}, u32[]{:S(2)}) %all-to-all-start.1) | async-done | bytes 2359328 | tf_op jit(solution)/shard_map/all_to_all | solution.py:70
  89.6 4.5 all-to-all-start
  94.1 0.2 all-reduce.4.cloned.1.call-start
  94.5 5.9 fusion.18
  100.4 8.1 %fusion.24 = f32[256,1536]{1,0:T(8,128)} fusion(), kind=kLoop, calls=%fused_computation.35 | loop fusion | flops 3538944 | bytes 1572864 | tf_op jit(solution)/shard_map/cos | solution.py:23
  108.5 6.8 fusion.21
  115.3 7.0 fusion.27
  122.4 1.8 copy.39
  124.2 1.7 copy.51
  125.9 21.7 %all-to-all-done = bf16[2,4,384,384]{3,1,0,2:T(4,128)(2,1)} async-done(((bf16[2,4,384,384]{3,1,0,2:T(4,128)(2,1)}), bf16[2,4,384,384]{3,1,0,2:T(4,128)(2,1)}, u32[]{:S(2)}, u32[]{:S(2)}) %all-to-all-start) | async-done | bytes 2359328 | tf_op jit(solution)/shard_map/all_to_all | solution.py:67
  147.6 5.7 copy.55
  153.2 6.4 reshape.157
  159.6 10.9 %fusion.47 = f32[2,4,96,512]{3,2,1,0:T(8,128)S(1)} fusion(f32[1536,256]{1,0:T(8,128)} %fusion.21, f32[1536,256]{1,0:T(8,128)S(1)} %fusion.18, f32[2,4,96,1536]{3,2,1,0:T(8,128)} %reshape.157, f32[4,96,1536]{2,1,0:T(8,128)} %bitcast.73, f32[4,512]{1,0:T(4,128)S(1)} %fusion.65), kind=kOutput, calls=%fused_computation.72 | convolution fusion | flops 7250903040 | bytes 11804672 | tf_op jit(solution)/shard_map/dot_general | solution.py:57
  170.6 8.8 %multiply_reduce_fusion.1 = f32[4,96,1536]{2,1,0:T(8,128)S(1)} fusion(f32[2,4,96,1536]{3,2,1,0:T(8,128)S(1)} %copy-done, f32[256,1536]{1,0:T(8,128)S(1)} %copy-done.10, f32[256,1536]{1,0:T(8,128)S(1)} %copy-done.8, f32[2,4,96,512]{3,2,1,0:T(8,128)S(1)} %fusion.47, f32[4,512]{1,0:T(4,128)S(1)} %fusion.65), kind=kOutput, calls=%fused_computation.11 | convolution fusion | flops 7251492864 | bytes 11804672 | tf_op jit(solution)/shard_map/dot_general | solution.py:81
  179.4 0.2 slice_bitcast_fusion.7
  179.6 0.2 pad_maximum_fusion
  179.8 55.9 %all_to_all.64 = f32[4,4,96,384]{3,2,1,0:T(8,128)S(1)} all-to-all(f32[4,4,96,384]{3,2,1,0:T(8,128)S(1)} %pad_maximum_fusion), channel_id=1, replica_groups=mesh['mem'=4,'lat'=2,'lon'=4] {'lon'}, dimensions={0} | all-to-all | bytes 4718592 | tf_op jit(solution)/shard_map/all_to_all | solution.py:90
  235.7 1.6 copy.41
  237.3 3.2 reshape.149
  240.6 54.8 %all-reduce.4.cloned.1.call-done = f32[589824]{0:T(1024)} async-done(((f32[589824]{0:T(1024)}), f32[589824]{0:T(1024)}) %all-reduce.4.cloned.1.call-update) | async-done | bytes 2359312 | tf_op jit(solution)/shard_map/psum | solution.py:36
  295.5 24.5 %gather_fusion = f32[2048]{0:T(1024)S(1)} fusion(f32[589824]{0:T(1024)} %all-reduce.4.cloned.1.call-done, s32[2048]{0:T(1024)S(1)} %broadcast_clamp_fusion), kind=kCustom, calls=%fused_computation | custom fusion | bytes 24576 | tf_op jit(solution)/shard_map/gather | solution.py:96
  320.0 12.8 %scatter_custom_fusion.1 = f32[589824]{0:T(1024)} fusion(s32[2048]{0:T(1024)S(1)} %bitcast.86, f32[2048]{0:T(1024)S(1)} %mul.226, f32[]{:T(128)} %constant.20.clone.1), kind=kCustom, calls=%fused_computation.75 | custom fusion | flops 2048 | bytes 2359300 | tf_op jit(solution)/shard_map/scatter-add | solution.py:53
  332.8 3.4 reshape.150
  336.2 3.2 copy.42
  339.4 58.7 %all_to_all.65 = f32[4,384,384]{2,0,1:T(4,128)S(1)} all-to-all(f32[4,384,384]{2,0,1:T(4,128)S(1)} %copy.42), channel_id=1, replica_groups=mesh['mem'=4,'lat'=2,'lon'=4] {'lon'}, dimensions={1} | all-to-all | bytes 4718592 | tf_op jit(solution)/shard_map/all_to_all | solution.py:70
  398.1 0.2 copy.43
  398.3 0.3 copy.52
  398.6 0.5 slice-done.1
  399.1 0.6 copy-done.2
  399.7 0.5 copy-done.4
  400.2 8.6 %multiply_reduce_fusion.4 = (f32[]{:T(128)}, f32[]{:T(128)}, f32[2,4,96,512]{3,2,1,0:T(8,128)S(1)}) fusion(f32[2,4,96,512]{3,2,1,0:T(8,128)S(1)} %fusion.47, f32[4,512]{1,0:T(4,128)S(1)} %fusion.65, f32[1536,256]{1,0:T(8,128)S(1)} %copy-done.4, f32[1536,256]{1,0:T(8,128)S(1)} %copy-done.2, f32[2,4,96,1536]{3,2,1,0:T(8,128)S(1)} %bitcast.69, ...), kind=kOutput, calls=%fused_computation.47 | convolution fusion | flops 7252869120 | bytes 13377544 | tf_op jit(solution)/shard_map/dot_general | solution.py:57
  408.8 38.4 %all-reduce = (f32[]{:T(128)}, f32[]{:T(128)}) all-reduce(f32[]{:T(128)} %get-tuple-element.3, f32[]{:T(128)} %get-tuple-element.2), channel_id=1, replica_groups=mesh['mem'=4,'lat'=2,'lon'=4] {'mem','lat','lon'}, use_global_device_ids=true, to_apply=%region_2.3 | all-reduce | flops 2 | bytes 16 | tf_op jit(solution)/shard_map/psum | solution.py:40
  448.3 1.0 multiply_reduce_fusion.3
  449.3 41.4 %psum.45 = f32[]{:T(128)} all-reduce(f32[]{:T(128)} %multiply_reduce_fusion.3), channel_id=1, replica_groups=mesh['mem'=4,'lat'=2,'lon'=4] {'mem','lat','lon'}, use_global_device_ids=true, to_apply=%region_9.10 | all-reduce | flops 1 | bytes 8 | tf_op jit(solution)/shard_map/psum | solution.py:40
  491.9 0.4 multiply_add_fusion.2
  492.3 1.0 copy-done.9
  493.3 0.5 copy-done.11
  493.7 10.5 %multiply_reduce_fusion = f32[4,96,1536]{2,1,0:T(8,128)S(1)} fusion(f32[2,4,96,1536]{3,2,1,0:T(8,128)} %reshape.157, f32[256,1536]{1,0:T(8,128)S(1)} %copy-done.11, f32[256,1536]{1,0:T(8,128)S(1)} %copy-done.9, f32[2,4,96,512]{3,2,1,0:T(8,128)S(1)} %multiply_add_fusion.2, f32[4,512]{1,0:T(4,128)S(1)} %fusion.65), kind=kOutput, calls=%fused_computation.8 | convolution fusion | flops 7251492864 | bytes 11804672 | tf_op jit(solution)/shard_map/dot_general | solution.py:81
  504.3 0.2 slice_bitcast_fusion.3
  504.5 0.2 pad_maximum_fusion.1
  504.7 55.9 %all_to_all.66 = f32[4,4,96,384]{3,2,1,0:T(8,128)S(1)} all-to-all(f32[4,4,96,384]{3,2,1,0:T(8,128)S(1)} %pad_maximum_fusion.1), channel_id=1, replica_groups=mesh['mem'=4,'lat'=2,'lon'=4] {'lon'}, dimensions={0} | all-to-all | bytes 4718592 | tf_op jit(solution)/shard_map/all_to_all | solution.py:90
  560.6 1.6 copy.45
  562.2 3.2 reshape.153
  565.5 54.8 %all-reduce.6.cloned.1.call-done = f32[589824]{0:T(1024)} async-done(((f32[589824]{0:T(1024)}), f32[589824]{0:T(1024)}) %all-reduce.6.cloned.1.call-update) | async-done | bytes 2359312 | tf_op jit(solution)/shard_map/psum | solution.py:36
  620.2 24.5 %gather_fusion.1 = f32[2048]{0:T(1024)S(1)} fusion(f32[589824]{0:T(1024)} %all-reduce.6.cloned.1.call-done, s32[2048]{0:T(1024)S(1)} %broadcast_clamp_fusion), kind=kCustom, calls=%fused_computation.1 | custom fusion | bytes 24576 | tf_op jit(solution)/shard_map/gather | solution.py:96
  644.7 12.8 %scatter_custom_fusion.2 = f32[589824]{0:T(1024)} fusion(s32[2048]{0:T(1024)S(1)} %bitcast.87, f32[2048]{0:T(1024)S(1)} %mul.240, f32[]{:T(128)} %constant.20.clone.1), kind=kCustom, calls=%fused_computation.73 | custom fusion | flops 2048 | bytes 2359300 | tf_op jit(solution)/shard_map/scatter-add | solution.py:53
  657.5 3.4 reshape.154
  661.0 3.2 copy.46
  664.2 58.4 %all_to_all.67 = f32[4,384,384]{2,0,1:T(4,128)S(1)} all-to-all(f32[4,384,384]{2,0,1:T(4,128)S(1)} %copy.46), channel_id=1, replica_groups=mesh['mem'=4,'lat'=2,'lon'=4] {'lon'}, dimensions={1} | all-to-all | bytes 4718592 | tf_op jit(solution)/shard_map/all_to_all | solution.py:70
  722.8 0.3 copy.53
  723.1 0.5 slice-done.3
  723.6 0.6 copy-done.3
  724.2 0.5 copy-done.5
  724.7 0.5 copy-done.7
  725.2 9.5 %multiply_reduce_fusion.2 = (f32[]{:T(128)}, f32[2,4,96,512]{3,2,1,0:T(8,128)}) fusion(f32[2,4,96,512]{3,2,1,0:T(8,128)S(1)} %copy-done.7, f32[4,512]{1,0:T(4,128)S(1)} %fusion.65, f32[1536,256]{1,0:T(8,128)S(1)} %copy-done.5, f32[1536,256]{1,0:T(8,128)S(1)} %copy-done.3, f32[2,4,96,1536]{3,2,1,0:T(8,128)S(1)} %bitcast.71, f32[4,96,1536]{2,1,0:T(8,128)S(1)} %bitcast.74), kind=kOutput, calls=%fused_computation.41 | convolution fusion | flops 7252082688 | bytes 13377540 | tf_op jit(solution)/shard_map/dot_general | solution.py:57
  734.7 38.3 %psum.47 = f32[]{:T(128)} all-reduce(f32[]{:T(128)} %get-tuple-element.17), channel_id=1, replica_groups=mesh['mem'=4,'lat'=2,'lon'=4] {'mem','lat','lon'}, use_global_device_ids=true, to_apply=%region_14.15 | all-reduce | flops 1 | bytes 8 | tf_op jit(solution)/shard_map/psum | solution.py:98
  774.2 4.3 multiply_subtract_fusion
  (42 shorter events, 0.4 us)
Async XLA Ops:
  29.4 60.3 %all-to-all-start.1 = ((f32[4,384,384]{2,0,1:T(4,128)}), f32[4,384,384]{2,0,1:T(4,128)}, u32[]{:S(2)}, u32[]{:S(2)}) async-start(f32[4,384,384]{2,0,1:T(4,128)} %copy.38), calls=%async_computation.1 | async-start | bytes 4718592 | tf_op jit(solution)/shard_map/all_to_all | solution.py:70
  40.6 53.8 %copy-start.13 = (s32[4]{0:T(128)S(1)}, s32[4]{0:T(128)}, u32[]{:S(2)}) copy-start(s32[4]{0:T(128)} %param.11) | copy-start | bytes 52
  89.6 57.9 %all-to-all-start = ((bf16[2,4,384,384]{3,1,0,2:T(4,128)(2,1)}), bf16[2,4,384,384]{3,1,0,2:T(4,128)(2,1)}, u32[]{:S(2)}, u32[]{:S(2)}) async-start(bf16[2,4,384,384]{3,1,0,2:T(4,128)(2,1)} %copy.36), calls=%async_computation | async-start | bytes 4718592 | tf_op jit(solution)/shard_map/all_to_all | solution.py:67
  94.1 201.3 %all-reduce.4.cloned.1.call-start = ((), (), s32[]{:S(2)}) async-start(), calls=%async_computation.6 | async-start | bytes 4718592 | tf_op jit(solution)/shard_map/psum | solution.py:36
  100.4 59.2 %copy-start.1 = (f32[1536,256]{1,0:T(8,128)}, f32[1536,256]{1,0:T(8,128)S(1)}, u32[]{:S(2)}) copy-start(f32[1536,256]{1,0:T(8,128)S(1)} %fusion.18) | copy-start | bytes 4718596
  159.6 10.9 %copy-start = (f32[2,4,96,1536]{3,2,1,0:T(8,128)S(1)}, f32[2,4,96,1536]{3,2,1,0:T(8,128)}, u32[]{:S(2)}) copy-start(f32[2,4,96,1536]{3,2,1,0:T(8,128)} %reshape.157) | copy-start | bytes 14155780
  159.6 10.9 %copy-start.8 = (f32[256,1536]{1,0:T(8,128)S(1)}, f32[256,1536]{1,0:T(8,128)}, u32[]{:S(2)}) copy-start(f32[256,1536]{1,0:T(8,128)} %fusion.24) | copy-start | bytes 4718596
  159.6 11.0 %copy-start.10 = (f32[256,1536]{1,0:T(8,128)S(1)}, f32[256,1536]{1,0:T(8,128)}, u32[]{:S(2)}) copy-start(f32[256,1536]{1,0:T(8,128)} %fusion.27) | copy-start | bytes 4718596
  240.6 379.7 %all-reduce.6.cloned.1.call-start = ((), (), s32[]{:S(2)}) async-start(), calls=%async_computation.7 | async-start | bytes 4718592 | tf_op jit(solution)/shard_map/psum | solution.py:36
  240.6 79.3 %copy-start.12 = (f32[1,2048]{1,0:T(1,128)S(1)}, f32[1,2048]{1,0:T(1,128)}, u32[]{:S(2)}) copy-start(f32[1,2048]{1,0:T(1,128)} %param.8) | copy-start | bytes 24580
  339.4 59.2 %slice-start = ((s8[4718592]{0:T(1024)(128)(4,1)}), s8[4194304]{0:T(1024)(128)(4,1)S(1)}, s32[]{:S(2)}) async-start(s8[4718592]{0:T(1024)(128)(4,1)} %bitcast.68), calls=%async_computation.8 | async-start | bytes 8388608
  398.1 1.0 slice-start.1
  398.2 1.4 copy-start.2
  398.3 1.9 copy-start.4
  491.9 1.4 copy-start.9
  491.9 1.9 copy-start.11
  493.7 10.5 %copy-start.6 = (f32[2,4,96,512]{3,2,1,0:T(8,128)}, f32[2,4,96,512]{3,2,1,0:T(8,128)S(1)}, u32[]{:S(2)}) copy-start(f32[2,4,96,512]{3,2,1,0:T(8,128)S(1)} %multiply_add_fusion.2) | copy-start | bytes 4718596
  664.1 59.0 %slice-start.2 = ((s8[4718592]{0:T(1024)(128)(4,1)}), s8[4194304]{0:T(1024)(128)(4,1)S(1)}, s32[]{:S(2)}) async-start(s8[4718592]{0:T(1024)(128)(4,1)} %bitcast.70), calls=%async_computation.10 | async-start | bytes 8388608
  722.6 1.0 slice-start.3
  722.8 1.4 copy-start.3
  722.8 1.9 copy-start.5
  722.8 2.4 copy-start.7
Sparse Core Ops, SparseCore 0:
  240.7 54.7 all-reduce.3
  565.6 54.5 all-reduce.5
